TPU v7x, 32 devices: a whole 2x2x4 slice. The times are simulated.
32 devices in a mesh: dp: 4 (over z), seq: 2 (over x), tensor: 4 (over y, core).
Axes of the slice: x: 2, y: 2, z: 4, core: 2. Of those that a mesh axis runs over, the one named last changes fastest.
Arguments:
- inputs: bfloat16 [4, 4096, 768], P('dp', 'seq'), may hold values from -6 to 6
- pass_embed: float32 [768], replicated, may hold values from -3 to 3
- norm1_gain: float32 [768], replicated, may hold values from 0.5 to 1.5
- norm1_shift: float32 [768], replicated, may hold values from -1 to 1
- w_qkv: bfloat16 [3, 768, 768], P(None, None, 'tensor'), may hold values from -0.21875 to 0.21875
- b_qv: float32 [2, 768], P(None, 'tensor'), may hold values from -1 to 1
- w_out: bfloat16 [768, 768], P('tensor'), may hold values from -0.875 to 0.875
- b_out: float32 [768], replicated, may hold values from -1 to 1
- norm2_gain: float32 [768], replicated, may hold values from 0.5 to 1.5
- norm2_shift: float32 [768], replicated, may hold values from -1 to 1
- w_up: bfloat16 [768, 3072], P(None, 'tensor'), may hold values from -0.21875 to 0.21875
- b_up: float32 [3072], P('tensor'), may hold values from -1.5 to 1.5
- w_down: bfloat16 [3072, 768], P('tensor'), may hold values from -0.109375 to 0.109375
- b_down: float32 [768], replicated, may hold values from -1 to 1
- out_grad: bfloat16 [4, 4096, 768], P('dp', 'seq'), may hold values from -6 to 6
- seg_id: int32 [4, 4096], P('dp'), may hold values from 0 to 12, as said below
- parent: int32 [4, 13], P('dp'), may hold values from 0 to 4, as said below
Outputs:
- output: bfloat16 [4, 4096, 768], P('dp', ('seq', 'tensor'))
- input_grad: bfloat16 [4, 4096, 768], P('dp', ('seq', 'tensor'))
- grad_pass: float32 [768], replicated
- grad_norm1_gain: float32 [768], replicated
- grad_norm1_shift: float32 [768], replicated
- grad_w_qkv: float32 [3, 768, 768], P(None, None, 'tensor')
- grad_b_qv: float32 [2, 768], P(None, 'tensor')
- grad_w_out: float32 [768, 768], P('tensor')
- grad_b_out: float32 [768], replicated
- grad_norm2_gain: float32 [768], replicated
- grad_norm2_shift: float32 [768], replicated
- grad_w_up: float32 [768, 3072], P(None, 'tensor')
- grad_b_up: float32 [3072], P('tensor')
- grad_w_down: float32 [3072, 768], P('tensor')
- grad_b_down: float32 [768], replicated
Inputs may be any that keep to these rules, and one draw needn't show every extreme that they name: `seg_id`: in each tree segment 0 (the trunk) covers 1024 consecutive tokens starting at a multiple of 1024; each other segment covers 256 consecutive tokens starting at a multiple of 256. Segment 0 is its own parent; segments 1 to 4 have parent 0; each of them is the parent of exactly two of the other segments.
All inputs are finite; a program needn't handle non-finite values.
Results may differ from a plain program's by a relative error of at most 0.019.
Values may be sent and summed in bfloat16 or wider, within the bound.
No kernel may reach another device: no remote copies, remote signals or barrier semaphores. Data moves between devices by JAX's collectives and lax.ppermute only.
A program may use at most 256 MiB of HBM per device.

v0:
```python
import jax
import jax.numpy as jnp
from jax import lax
from jax.sharding import PartitionSpec as P

HD = 64
EPS = 1e-05
ROOT = 0.7978845608028654


def norm_stats(values):
    row_mean = jnp.mean(values, -1, keepdims=True)
    centred = values - row_mean
    inv_std = lax.rsqrt(jnp.mean(centred * centred, -1, keepdims=True) + EPS)
    return (centred * inv_std, inv_std)


def norm_back(grad_out, normal, inv_std, gain_vec):
    scaled = grad_out * gain_vec
    return inv_std * (
        scaled
        - jnp.mean(scaled, -1, keepdims=True)
        - normal * jnp.mean(scaled * normal, -1, keepdims=True)
    )


def gelu_parts(pre_act):
    cubic_term = 0.044715 * pre_act * pre_act * pre_act
    tangent = jnp.tanh(ROOT * (pre_act + cubic_term))
    gelu_value = 0.5 * pre_act * (1.0 + tangent)
    gelu_slope = 0.5 * (1.0 + tangent) + 0.5 * pre_act * (1.0 - tangent * tangent) * ROOT * (
        1.0 + 3.0 * 0.044715 * pre_act * pre_act
    )
    return (gelu_value, gelu_slope)


def forward_rows(left, right):
    return jnp.einsum("tbd,de->tbe", left, right, preferred_element_type=jnp.float32)


def weight_grad(left, right):
    return jnp.einsum("tbd,tbe->de", left, right, preferred_element_type=jnp.float32)


def input_rows(grad_rows, weight):
    return jnp.einsum("tbe,de->tbd", grad_rows, weight, preferred_element_type=jnp.float32)


def row_total(values):
    return jnp.sum(values.astype(jnp.float32), axis=(0, 1))


def ancestry(parent_row):
    labels = jnp.arange(parent_row.shape[0], dtype=jnp.int32)
    step_up = (
        (parent_row[:, None] == labels[None, :]) & (labels[:, None] != labels[None, :])
    ).astype(jnp.float32)
    return step_up + jnp.dot(step_up, step_up)


def visibility(seg_query, pos_query, seg_keys, ancestor):
    labels = jnp.arange(ancestor.shape[0], dtype=jnp.int32)
    query_hot = (seg_query[:, None] == labels[None, :]).astype(jnp.float32)
    key_hot = (labels[:, None] == seg_keys[None, :]).astype(jnp.float32)
    reachable = jnp.dot(jnp.dot(query_hot, ancestor), key_hot)
    key_pos = jnp.arange(seg_keys.shape[0], dtype=jnp.int32)
    same_seg = (seg_query[:, None] == seg_keys[None, :]) & (pos_query[:, None] >= key_pos[None, :])
    return same_seg | (reachable > 0.5)


def attend(queries, key_heads, value_heads, seg_row, ancestor, first_row):
    block_len = queries.shape[0]
    head_count = key_heads.shape[1]
    blk_width = min(512, block_len)
    blk_count = block_len // blk_width
    q_blocks = queries.reshape(blk_count, blk_width, head_count, HD)
    starts = first_row + blk_width * jnp.arange(blk_count, dtype=jnp.int32)

    def one_block(pieces):
        q_block, blk_start = pieces
        visible = visibility(
            lax.dynamic_slice_in_dim(seg_row, blk_start, blk_width),
            blk_start + jnp.arange(blk_width, dtype=jnp.int32),
            seg_row,
            ancestor,
        )
        scores = (
            jnp.einsum("qhd,khd->hqk", q_block, key_heads, preferred_element_type=jnp.float32)
            * 0.125
        )
        scores = jnp.where(visible[None], scores, -jnp.inf)
        row_top = jnp.max(scores, -1, keepdims=True)
        weights = jnp.exp(scores - row_top)
        row_sum = jnp.sum(weights, -1, keepdims=True)
        prob_low = (weights / row_sum).astype(jnp.bfloat16)
        mixture = jnp.einsum(
            "hqk,khd->qhd", prob_low, value_heads, preferred_element_type=jnp.float32
        )
        return (mixture, (row_top + jnp.log(row_sum))[..., 0])

    mixture, log_sums = lax.map(one_block, (q_blocks, starts))
    return (mixture.reshape(block_len, head_count * HD), log_sums)


def attend_back(queries, key_heads, value_heads, grad_mix, log_sums, seg_row, ancestor, first_row):
    block_len = queries.shape[0]
    head_count = key_heads.shape[1]
    blk_width = min(512, block_len)
    blk_count = block_len // blk_width
    q_blocks = queries.reshape(blk_count, blk_width, head_count, HD)
    g_blocks = grad_mix.reshape(blk_count, blk_width, head_count, HD)
    starts = first_row + blk_width * jnp.arange(blk_count, dtype=jnp.int32)

    def one_block(totals, pieces):
        q_block, g_block, lse_block, blk_start = pieces
        visible = visibility(
            lax.dynamic_slice_in_dim(seg_row, blk_start, blk_width),
            blk_start + jnp.arange(blk_width, dtype=jnp.int32),
            seg_row,
            ancestor,
        )
        scores = (
            jnp.einsum("qhd,khd->hqk", q_block, key_heads, preferred_element_type=jnp.float32)
            * 0.125
        )
        probs_full = jnp.where(visible[None], jnp.exp(scores - lse_block[..., None]), 0.0)
        grad_prob = jnp.einsum(
            "qhd,khd->hqk", g_block, value_heads, preferred_element_type=jnp.float32
        )
        inner = jnp.sum(probs_full * grad_prob, -1, keepdims=True)
        grad_score = (probs_full * (grad_prob - inner)).astype(jnp.bfloat16)
        grad_query = (
            jnp.einsum("hqk,khd->qhd", grad_score, key_heads, preferred_element_type=jnp.float32)
            * 0.125
        )
        key_sum = (
            totals[0]
            + jnp.einsum("hqk,qhd->khd", grad_score, q_block, preferred_element_type=jnp.float32)
            * 0.125
        )
        value_sum = totals[1] + jnp.einsum(
            "hqk,qhd->khd",
            probs_full.astype(jnp.bfloat16),
            g_block,
            preferred_element_type=jnp.float32,
        )
        totals = (key_sum, value_sum)
        return (totals, (grad_query, inner[..., 0]))

    zero_keys = jnp.zeros(key_heads.shape, jnp.float32)
    start_totals = (zero_keys, zero_keys)
    totals, (grad_query, inner) = lax.scan(
        one_block, start_totals, (q_blocks, g_blocks, log_sums, starts)
    )
    length = key_heads.shape[0]
    kv_term = None
    kv_term = jnp.concatenate(
        [totals[0].reshape(length, head_count * HD), totals[1].reshape(length, head_count * HD)], -1
    )
    return (grad_query.reshape(block_len, head_count * HD), inner, kv_term)


def local(
    inputs,
    pass_embed,
    norm1_gain,
    norm1_shift,
    w_qkv,
    b_qv,
    w_out,
    b_out,
    norm2_gain,
    norm2_shift,
    w_up,
    b_up,
    w_down,
    b_down,
    out_grad,
    seg_id,
    parent,
):
    tree_count = inputs.shape[0]
    block_len = inputs.shape[1]
    local_width = w_qkv.shape[2]
    head_count = local_width // HD
    sub_len = block_len // lax.axis_size("tensor")
    sub_start = lax.axis_index("tensor") * sub_len
    first_row = lax.axis_index("seq") * block_len

    def own_rows(values):
        return lax.dynamic_slice_in_dim(values, sub_start, sub_len, 1)

    residual = inputs.astype(jnp.float32) + pass_embed
    norm_one, inv_one = norm_stats(residual)
    normed = (norm_one * norm1_gain + norm1_shift).astype(jnp.bfloat16)
    queries = (forward_rows(normed, w_qkv[0]) + b_qv[0]).astype(jnp.bfloat16)
    key_loc = forward_rows(normed, w_qkv[1]).astype(jnp.bfloat16)
    value_loc = (forward_rows(normed, w_qkv[2]) + b_qv[1]).astype(jnp.bfloat16)
    gathered = lax.all_gather(jnp.concatenate([key_loc, value_loc], -1), "seq", axis=1, tiled=True)
    length = gathered.shape[1]
    key_all = gathered[..., :local_width].reshape(tree_count, length, head_count, HD)
    value_all = gathered[..., local_width:].reshape(tree_count, length, head_count, HD)
    ancestors = [ancestry(parent[0])]
    tree_idx = 0
    mixed_tree, log_sums = attend(
        queries[tree_idx],
        key_all[tree_idx],
        value_all[tree_idx],
        seg_id[tree_idx],
        ancestors[tree_idx],
        first_row,
    )
    mix_list = [mixed_tree]
    lse_list = [log_sums]
    mixture = jnp.stack(mix_list).astype(jnp.bfloat16)
    partial_attn = forward_rows(mixture, w_out)
    middle = (
        residual + lax.psum(partial_attn.astype(jnp.bfloat16), "tensor").astype(jnp.float32) + b_out
    )
    norm_two, inv_two = norm_stats(middle)
    lifted_own = (norm_two * norm2_gain + norm2_shift).astype(jnp.bfloat16)
    pre_act = forward_rows(lifted_own, w_up) + b_up
    gelu_value, gelu_slope = gelu_parts(pre_act)
    active = gelu_value.astype(jnp.bfloat16)
    partial_mlp = forward_rows(active, w_down)
    output = own_rows(
        middle + lax.psum(partial_mlp.astype(jnp.bfloat16), "tensor").astype(jnp.float32) + b_down
    ).astype(jnp.bfloat16)
    grad_w_down = weight_grad(active, out_grad)
    grad_b_down = row_total(out_grad)
    grad_pre = (input_rows(out_grad, w_down) * gelu_slope).astype(jnp.bfloat16)
    grad_w_up = weight_grad(lifted_own, grad_pre)
    grad_b_up = row_total(grad_pre)
    partial_lift = input_rows(grad_pre, w_up)
    grad_lift = lax.psum(partial_lift.astype(jnp.bfloat16), "tensor").astype(jnp.float32)
    grad_middle = out_grad.astype(jnp.float32) + norm_back(grad_lift, norm_two, inv_two, norm2_gain)
    grad_g2 = row_total(grad_lift * norm_two)
    grad_b2 = row_total(grad_lift)
    grad_b_out = row_total(grad_middle)
    proj_low = grad_middle.astype(jnp.bfloat16)
    grad_w_out = weight_grad(mixture, proj_low)
    grad_mix = input_rows(proj_low, w_out).astype(jnp.bfloat16)
    tree_idx = 0
    grad_query, inner, kv_term = attend_back(
        queries[tree_idx],
        key_all[tree_idx],
        value_all[tree_idx],
        grad_mix[tree_idx],
        lse_list[tree_idx],
        seg_id[tree_idx],
        ancestors[tree_idx],
        first_row,
    )
    query_list = [grad_query]
    term_list = [kv_term]
    kv_grads = lax.psum_scatter(
        jnp.stack(term_list).astype(jnp.bfloat16), "seq", scatter_dimension=1, tiled=True
    ).astype(jnp.float32)
    grad_q = jnp.stack(query_list).astype(jnp.bfloat16)
    grad_k = kv_grads[..., :local_width].astype(jnp.bfloat16)
    grad_v = kv_grads[..., local_width:].astype(jnp.bfloat16)
    grad_w_qkv = jnp.stack(
        [weight_grad(normed, grad_q), weight_grad(normed, grad_k), weight_grad(normed, grad_v)]
    )
    grad_b_qv = jnp.stack([row_total(grad_q), row_total(grad_v)])
    partial_norm = (
        input_rows(grad_q, w_qkv[0]) + input_rows(grad_k, w_qkv[1]) + input_rows(grad_v, w_qkv[2])
    )
    grad_norm = lax.psum(partial_norm.astype(jnp.bfloat16), "tensor").astype(jnp.float32)
    grad_resid = grad_middle + norm_back(grad_norm, norm_one, inv_one, norm1_gain)
    input_grad = own_rows(grad_resid).astype(jnp.bfloat16)
    grad_pass = row_total(grad_resid)
    grad_g1 = row_total(grad_norm * norm_one)
    grad_b1 = row_total(grad_norm)
    summed = lax.psum(
        (
            grad_w_qkv,
            grad_b_qv,
            grad_w_out,
            grad_w_up,
            grad_b_up,
            grad_w_down,
            grad_b_down,
            grad_pass,
            grad_g1,
            grad_b1,
            grad_g2,
            grad_b2,
            grad_b_out,
        ),
        ("dp", "seq"),
    )
    return (
        output,
        input_grad,
        summed[7],
        summed[8],
        summed[9],
        summed[0],
        summed[1],
        summed[2],
        summed[12],
        summed[10],
        summed[11],
        summed[3],
        summed[4],
        summed[5],
        summed[6],
    )


def solution(mesh):
    return jax.shard_map(
        local,
        mesh=mesh,
        in_specs=(
            P("dp", "seq", None),
            P(),
            P(),
            P(),
            P(None, None, "tensor"),
            P(None, "tensor"),
            P("tensor", None),
            P(),
            P(),
            P(),
            P(None, "tensor"),
            P("tensor"),
            P("tensor", None),
            P(),
            P("dp", "seq", None),
            P("dp", None),
            P("dp", None),
        ),
        out_specs=(
            P("dp", ("seq", "tensor"), None),
            P("dp", ("seq", "tensor"), None),
            P(),
            P(),
            P(),
            P(None, None, "tensor"),
            P(None, "tensor"),
            P("tensor", None),
            P(),
            P(),
            P(),
            P(None, "tensor"),
            P("tensor"),
            P("tensor", None),
            P(),
        ),
        check_vma=False,
    )
```

profile of v0, /device:TPU:0, one launch (start us, length us, event | category | flops | bytes accessed | tf_op | source)
XLA Modules:
  0.0 1257.9 jit_solution(2198636816615368359)
XLA Ops:
  23.9 43.7 %all-gather.2.cloned.1.call-done = bf16[1,4096,384]{1,2,0:T(8,128)(2,1)} async-done(((bf16[1,2048,384]{1,2,0:T(8,128)(2,1)}), bf16[1,4096,384]{1,2,0:T(8,128)(2,1)}) %all-gather.2.cloned.1.call-update) | async-done | bytes 3145744 | tf_op jit(solution)/shard_map/all_gather | solution.py:199
  71.8 184.3 %while.27 = (s32[]{:T(128)}, bf16[4,512,3,64]{1,3,2,0:T(8,128)(2,1)}, f32[4,3,512]{2,1,0:T(4,128)}, s32[4]{0:T(128)S(1)}, s32[4096]{0:T(1024)}, /*index=5*/s32[1...) while((s32[]{:T(128)}, ...), condition=%wide.region_5.6_spmd, body=%wide.region_2.5_spmd.sunk | while | flops 1751353856 | bytes 108675712 | solution.py:101
  81.2 12.1 fusion.191
  93.2 12.0 fusion.192
  105.2 12.1 fusion.193
  127.1 12.1 fusion.191
  139.2 12.0 fusion.192
  151.2 12.1 fusion.193
  173.1 12.1 fusion.191
  185.1 12.0 fusion.192
  197.1 12.1 fusion.193
  219.0 12.1 fusion.191
  231.1 12.0 fusion.192
  243.1 12.1 fusion.193
  262.8 68.4 %all-reduce.8.cloned.1.call-done = bf16[1,2048,768]{2,1,0:T(8,128)(2,1)} async-done(((bf16[1,2048,768]{2,1,0:T(8,128)(2,1)}), bf16[1,2048,768]{2,1,0:T(8,128)(2,1)}) %all-reduce.8.cloned.1.call-update) | async-done | bytes 3145744 | tf_op jit(solution)/shard_map/psum | solution.py:218
  353.9 68.6 %all-reduce.10.cloned.1.call-done = bf16[1,2048,768]{2,1,0:T(8,128)(2,1)} async-done(((bf16[1,2048,768]{2,1,0:T(8,128)(2,1)}), bf16[1,2048,768]{2,1,0:T(8,128)(2,1)}) %all-reduce.10.cloned.1.call-update) | async-done | bytes 3145744 | tf_op jit(solution)/shard_map/psum | solution.py:235
  445.2 377.5 %while.28 = (s32[]{:T(128)}, f32[4096,3,64]{0,2,1:T(8,128)}, f32[4096,3,64]{0,2,1:T(8,128)}, bf16[4,512,3,64]{1,3,2,0:T(8,128)(2,1)}, bf16[4,512,3,64]{1,3,2,0:T...) while((s32[]{:T(128)}, f32[4096,3,64]{0,2,1:T(8,128)}, ...), condition=%wide.region_15.16_spmd.clone, body=%wide.region_13.15_spmd.clone.sunk | while | flops 4190177792 | bytes 234558224 | solution.py:152
  453.9 13.3 %fusion.205 = f32[3,512,4096]{2,1,0:T(8,128)} fusion(bf16[4096,3,64]{0,2,1:T(8,128)(2,1)} %copy-done.1, bf16[4,512,3,64]{1,3,2,0:T(8,128)(2,1)} %copy-done.15, s32[]{:T(128)S(6)} %copy.60), kind=kOutput, calls=%fused_computation.48.clone.1 | convolution fusion | flops 805306368 | bytes 26935300 | tf_op jit(solution)/shard_map/while/body/eval_jaxpr/qhd,khd->hqk/dot_general | solution.py:123
  467.2 12.5 fusion.208
  479.8 18.3 %multiply_reduce_fusion.4 = (f32[3,512]{1,0:T(4,128)S(1)}, f32[3,512,4096]{2,1,0:T(8,128)}) fusion(f32[3,512,4096]{2,1,0:T(8,128)} %fusion.205, f32[3,512]{1,0:T(4,128)S(1)} %dynamic-slice_bitcast_fusion.2, pred[512,4096]{1,0:T(8,128)(4,1)S(1)} %fusion.206, bf16[4096,3,64]{0,2,1:T(8,128)(2,1)} %get-tuple-element.551, ...), kind=kOutput, calls=%fused_computation.25.clone.1 | convolution fusion | flops 836762112 | bytes 54210564 | tf_op jit(solution)/shard_map/while/body/eval_jaxpr/qhd,khd->hqk/dot_general | solution.py:127
  498.1 21.9 %multiply_convert_fusion.5 = bf16[3,512,4096]{2,1,0:T(8,128)(2,1)} fusion(f32[3,512,4096]{2,1,0:T(8,128)} %get-tuple-element.466, f32[3,512,4096]{2,1,0:T(8,128)} %fusion.205, f32[3,512]{1,0:T(4,128)S(1)} %get-tuple-element.467, f32[3,512]{1,0:T(4,128)S(1)} %dynamic-slice_bitcast_fusion.2, pred[512,4096]{1,0:T(8,128)(4,1)S(1)} %fusion.206), kind=kLoop, calls=%fused_computation.24.clone.1 | loop fusion | flops 37748736 | bytes 65024000 | tf_op jit(solution)/shard_map/while/body/eval_jaxpr/convert_element_type | solution.py:131
  520.0 9.7 fusion.209
  529.7 8.7 fusion.207
  546.7 13.3 %fusion.205 = f32[3,512,4096]{2,1,0:T(8,128)} fusion(bf16[4096,3,64]{0,2,1:T(8,128)(2,1)} %copy-done.1, bf16[4,512,3,64]{1,3,2,0:T(8,128)(2,1)} %copy-done.15, s32[]{:T(128)S(6)} %copy.60), kind=kOutput, calls=%fused_computation.48.clone.1 | convolution fusion | flops 805306368 | bytes 26935300 | tf_op jit(solution)/shard_map/while/body/eval_jaxpr/qhd,khd->hqk/dot_general | solution.py:123
  560.0 13.6 %fusion.208 = f32[4096,3,64]{0,2,1:T(8,128)} fusion(f32[3,512,4096]{2,1,0:T(8,128)} %fusion.205, f32[3,512]{1,0:T(4,128)S(1)} %dynamic-slice_bitcast_fusion.2, pred[512,4096]{1,0:T(8,128)(4,1)S(1)} %fusion.206, f32[4096,3,64]{0,2,1:T(8,128)} %get-tuple-element.525, pred[]{:T(512)S(6)} %compare.3, bf16[4,512,3,64]{1,3,2,0:T(8,128)(2,1)} %get-tuple-element.550, ...), kind=kOutput, calls=%fused_computation.37.clone.1 | convolution fusion | flops 832045056 | bytes 33757188 | tf_op jit(solution)/shard_map/while/body/eval_jaxpr/hqk,qhd->khd/dot_general | solution.py:141
  573.6 18.3 %multiply_reduce_fusion.4 = (f32[3,512]{1,0:T(4,128)S(1)}, f32[3,512,4096]{2,1,0:T(8,128)}) fusion(f32[3,512,4096]{2,1,0:T(8,128)} %fusion.205, f32[3,512]{1,0:T(4,128)S(1)} %dynamic-slice_bitcast_fusion.2, pred[512,4096]{1,0:T(8,128)(4,1)S(1)} %fusion.206, bf16[4096,3,64]{0,2,1:T(8,128)(2,1)} %get-tuple-element.551, ...), kind=kOutput, calls=%fused_computation.25.clone.1 | convolution fusion | flops 836762112 | bytes 54210564 | tf_op jit(solution)/shard_map/while/body/eval_jaxpr/qhd,khd->hqk/dot_general | solution.py:127
  591.9 21.9 %multiply_convert_fusion.5 = bf16[3,512,4096]{2,1,0:T(8,128)(2,1)} fusion(f32[3,512,4096]{2,1,0:T(8,128)} %get-tuple-element.466, f32[3,512,4096]{2,1,0:T(8,128)} %fusion.205, f32[3,512]{1,0:T(4,128)S(1)} %get-tuple-element.467, f32[3,512]{1,0:T(4,128)S(1)} %dynamic-slice_bitcast_fusion.2, pred[512,4096]{1,0:T(8,128)(4,1)S(1)} %fusion.206), kind=kLoop, calls=%fused_computation.24.clone.1 | loop fusion | flops 37748736 | bytes 65024000 | tf_op jit(solution)/shard_map/while/body/eval_jaxpr/convert_element_type | solution.py:131
  613.8 9.7 fusion.209
  623.5 9.6 fusion.207
  641.5 13.3 %fusion.205 = f32[3,512,4096]{2,1,0:T(8,128)} fusion(bf16[4096,3,64]{0,2,1:T(8,128)(2,1)} %copy-done.1, bf16[4,512,3,64]{1,3,2,0:T(8,128)(2,1)} %copy-done.15, s32[]{:T(128)S(6)} %copy.60), kind=kOutput, calls=%fused_computation.48.clone.1 | convolution fusion | flops 805306368 | bytes 26935300 | tf_op jit(solution)/shard_map/while/body/eval_jaxpr/qhd,khd->hqk/dot_general | solution.py:123
  654.7 13.6 %fusion.208 = f32[4096,3,64]{0,2,1:T(8,128)} fusion(f32[3,512,4096]{2,1,0:T(8,128)} %fusion.205, f32[3,512]{1,0:T(4,128)S(1)} %dynamic-slice_bitcast_fusion.2, pred[512,4096]{1,0:T(8,128)(4,1)S(1)} %fusion.206, f32[4096,3,64]{0,2,1:T(8,128)} %get-tuple-element.525, pred[]{:T(512)S(6)} %compare.3, bf16[4,512,3,64]{1,3,2,0:T(8,128)(2,1)} %get-tuple-element.550, ...), kind=kOutput, calls=%fused_computation.37.clone.1 | convolution fusion | flops 832045056 | bytes 33757188 | tf_op jit(solution)/shard_map/while/body/eval_jaxpr/hqk,qhd->khd/dot_general | solution.py:141
  668.4 18.3 %multiply_reduce_fusion.4 = (f32[3,512]{1,0:T(4,128)S(1)}, f32[3,512,4096]{2,1,0:T(8,128)}) fusion(f32[3,512,4096]{2,1,0:T(8,128)} %fusion.205, f32[3,512]{1,0:T(4,128)S(1)} %dynamic-slice_bitcast_fusion.2, pred[512,4096]{1,0:T(8,128)(4,1)S(1)} %fusion.206, bf16[4096,3,64]{0,2,1:T(8,128)(2,1)} %get-tuple-element.551, ...), kind=kOutput, calls=%fused_computation.25.clone.1 | convolution fusion | flops 836762112 | bytes 54210564 | tf_op jit(solution)/shard_map/while/body/eval_jaxpr/qhd,khd->hqk/dot_general | solution.py:127
  686.7 21.9 %multiply_convert_fusion.5 = bf16[3,512,4096]{2,1,0:T(8,128)(2,1)} fusion(f32[3,512,4096]{2,1,0:T(8,128)} %get-tuple-element.466, f32[3,512,4096]{2,1,0:T(8,128)} %fusion.205, f32[3,512]{1,0:T(4,128)S(1)} %get-tuple-element.467, f32[3,512]{1,0:T(4,128)S(1)} %dynamic-slice_bitcast_fusion.2, pred[512,4096]{1,0:T(8,128)(4,1)S(1)} %fusion.206), kind=kLoop, calls=%fused_computation.24.clone.1 | loop fusion | flops 37748736 | bytes 65024000 | tf_op jit(solution)/shard_map/while/body/eval_jaxpr/convert_element_type | solution.py:131
  708.6 9.7 fusion.209
  718.3 9.6 fusion.207
  736.2 13.3 %fusion.205 = f32[3,512,4096]{2,1,0:T(8,128)} fusion(bf16[4096,3,64]{0,2,1:T(8,128)(2,1)} %copy-done.1, bf16[4,512,3,64]{1,3,2,0:T(8,128)(2,1)} %copy-done.15, s32[]{:T(128)S(6)} %copy.60), kind=kOutput, calls=%fused_computation.48.clone.1 | convolution fusion | flops 805306368 | bytes 26935300 | tf_op jit(solution)/shard_map/while/body/eval_jaxpr/qhd,khd->hqk/dot_general | solution.py:123
  749.5 13.6 %fusion.208 = f32[4096,3,64]{0,2,1:T(8,128)} fusion(f32[3,512,4096]{2,1,0:T(8,128)} %fusion.205, f32[3,512]{1,0:T(4,128)S(1)} %dynamic-slice_bitcast_fusion.2, pred[512,4096]{1,0:T(8,128)(4,1)S(1)} %fusion.206, f32[4096,3,64]{0,2,1:T(8,128)} %get-tuple-element.525, pred[]{:T(512)S(6)} %compare.3, bf16[4,512,3,64]{1,3,2,0:T(8,128)(2,1)} %get-tuple-element.550, ...), kind=kOutput, calls=%fused_computation.37.clone.1 | convolution fusion | flops 832045056 | bytes 33757188 | tf_op jit(solution)/shard_map/while/body/eval_jaxpr/hqk,qhd->khd/dot_general | solution.py:141
  763.1 18.3 %multiply_reduce_fusion.4 = (f32[3,512]{1,0:T(4,128)S(1)}, f32[3,512,4096]{2,1,0:T(8,128)}) fusion(f32[3,512,4096]{2,1,0:T(8,128)} %fusion.205, f32[3,512]{1,0:T(4,128)S(1)} %dynamic-slice_bitcast_fusion.2, pred[512,4096]{1,0:T(8,128)(4,1)S(1)} %fusion.206, bf16[4096,3,64]{0,2,1:T(8,128)(2,1)} %get-tuple-element.551, ...), kind=kOutput, calls=%fused_computation.25.clone.1 | convolution fusion | flops 836762112 | bytes 54210564 | tf_op jit(solution)/shard_map/while/body/eval_jaxpr/qhd,khd->hqk/dot_general | solution.py:127
  781.4 21.9 %multiply_convert_fusion.5 = bf16[3,512,4096]{2,1,0:T(8,128)(2,1)} fusion(f32[3,512,4096]{2,1,0:T(8,128)} %get-tuple-element.466, f32[3,512,4096]{2,1,0:T(8,128)} %fusion.205, f32[3,512]{1,0:T(4,128)S(1)} %get-tuple-element.467, f32[3,512]{1,0:T(4,128)S(1)} %dynamic-slice_bitcast_fusion.2, pred[512,4096]{1,0:T(8,128)(4,1)S(1)} %fusion.206), kind=kLoop, calls=%fused_computation.24.clone.1 | loop fusion | flops 37748736 | bytes 65024000 | tf_op jit(solution)/shard_map/while/body/eval_jaxpr/convert_element_type | solution.py:131
  803.3 9.7 fusion.209
  813.0 9.6 fusion.207
  829.1 8.6 fusion.90
  843.1 29.5 %reduce-scatter.2.cloned.1.call-done = bf16[1,2048,384]{1,2,0:T(8,128)(2,1)} async-done(((bf16[1,4096,384]{1,2,0:T(8,128)(2,1)}), bf16[1,2048,384]{1,2,0:T(8,128)(2,1)}) %reduce-scatter.2.cloned.1.call-update) | async-done | bytes 1572880 | tf_op jit(solution)/shard_map/reduce_scatter | solution.py:256
  880.2 7.1 fusion.132
  887.3 7.9 fusion.86
  902.4 97.5 %all-reduce.14.cloned.1.call-done = (bf16[1,2048,768]{2,1,0:T(8,128)(2,1)}, bf16[1,2048,768]{2,1,0:T(8,128)(2,1)}) async-done(((bf16[1,2048,768]{2,1,0:T(8,128)(2,1)}, bf16[1,2048,768]{2,1,0:T(8,128)(2,1)}), (bf16[1,2048,768]{2,1,0:T(8,128)(2,1)}, bf16[1,2048,768]{2,1,0:T(8,128)(2,1)})) %all-reduce.14.cloned.1.call-update) | async-done | bytes 6291472 | tf_op jit(solution)/shard_map/psum | solution.py:227
  1011.9 41.2 %all-reduce = (f32[768]{0:T(1024)}, f32[768]{0:T(1024)}, f32[768]{0:T(1024)}, f32[2,192]{1,0:T(2,128)}, f32[768]{0:T(1024)}, /*index=5*/f32[768]{0:T(1024)}, f32[768]{0:T(1024)}, f32[768]{0:T(1024)}, f32[768]{0:T(1024)}) all-reduce(f32[768]{0:T(1024)S(1)} %get-tuple-element.301, ...), channel_id=1, replica_groups=mesh['dp'=4,'seq'=2,'tensor'=4] {'dp','seq'}, use_global_device_ids=true, to_apply=%region_21.22 | all-reduce | flops 6528 | bytes 52224 | tf_op jit(solution)/shard_map/psum | solution.py:275
  1058.1 185.1 %all-reduce.12.cloned.1.call-done = (f32[3,768,192]{1,2,0:T(8,128)}, f32[192,768]{1,0:T(8,128)}, f32[768,768]{1,0:T(8,128)}, f32[768,768]{1,0:T(8,128)}) async-done(((f32[3,768,192]{1,2,0:T(8,128)}, f32[192,768]{1,0:T(8,128)}, f32[768,768]{1,0:T(8,128)}, f32[768,768]{1,0:T(8,128)}), (f32[3,768,192]{1,2,0:T(8,128)}, f32[192,768]{1,0:T(8,128)}, f32[768,768]{1,0:T(8,128)}, ...) | async-done | bytes 7077904 | tf_op jit(solution)/shard_map/psum | solution.py:275
  (297 shorter events, 180.3 us)
Async XLA Ops:
  7.2 334.1 %copy-start = (bf16[768,768]{1,0:T(8,128)(2,1)S(1)}, bf16[768,768]{1,0:T(8,128)(2,1)}, u32[]{:S(2)}) copy-start(bf16[768,768]{1,0:T(8,128)(2,1)} %param.33) | copy-start | bytes 3538948
  7.2 60.3 %all-gather.2.cloned.1.call-start = ((), (), s32[]{:S(2)}) async-start(), calls=%async_computation.1 | async-start | bytes 4718592 | tf_op jit(solution)/shard_map/all_gather | solution.py:199
  8.1 8.0 copy-start.29
  19.8 311.5 %all-reduce.8.cloned.1.call-start = ((), (), s32[]{:S(2)}) async-start(), calls=%async_computation.2 | async-start | bytes 6291456 | tf_op jit(solution)/shard_map/psum | solution.py:218
  81.1 12.1 copy-start.8
  93.2 12.0 copy-start.7
  93.2 12.0 copy-start.24
  127.1 12.1 copy-start.8
  139.2 12.0 copy-start.7
  139.2 12.0 copy-start.24
  173.1 12.1 copy-start.8
  185.1 12.0 copy-start.7
  185.1 12.0 copy-start.24
  219.0 12.1 copy-start.8
  231.1 12.0 copy-start.7
  231.1 12.0 copy-start.24
  256.1 79.3 %copy-start.55 = (s32[4]{0:T(128)}, s32[4]{0:T(128)S(1)}, u32[]{:S(2)}) copy-start(s32[4]{0:T(128)S(1)} %get-tuple-element.618) | copy-start | bytes 52
  256.1 79.3 %copy-start.58 = (bf16[13,13]{1,0:T(8,128)(2,1)}, bf16[13,13]{1,0:T(8,128)(2,1)S(1)}, u32[]{:S(2)}) copy-start(bf16[13,13]{1,0:T(8,128)(2,1)S(1)} %get-tuple-element.636) | copy-start | bytes 1018
  256.1 75.2 %copy-start.34 = (f32[768]{0:T(1024)S(1)}, f32[768]{0:T(1024)}, u32[]{:S(2)}) copy-start(f32[768]{0:T(1024)} %param.22) | copy-start | bytes 9220
  256.1 75.2 %copy-start.46 = (f32[768]{0:T(1024)S(1)}, f32[768]{0:T(1024)}, u32[]{:S(2)}) copy-start(f32[768]{0:T(1024)} %param.28) | copy-start | bytes 9220
  262.6 159.9 %all-reduce.10.cloned.1.call-start = ((), (), s32[]{:S(2)}) async-start(), calls=%async_computation.3 | async-start | bytes 6291456 | tf_op jit(solution)/shard_map/psum | solution.py:235
  353.8 518.8 %reduce-scatter.2.cloned.1.call-start = ((), (), s32[]{:S(2)}) async-start(), calls=%async_computation.4 | async-start | bytes 4718592 | tf_op jit(solution)/shard_map/reduce_scatter | solution.py:256
  428.5 8.6 copy-start.30
  434.5 10.8 copy-start.56
  520.0 9.7 copy-start.16
  529.6 8.7 copy-start.2
  529.6 8.7 copy-start.57
  613.8 9.7 copy-start.16
  623.5 9.6 copy-start.2
  623.5 9.6 copy-start.57
  708.6 9.7 copy-start.16
  718.3 9.6 copy-start.2
  718.3 9.6 copy-start.57
  803.3 9.7 copy-start.16
  813.0 9.6 copy-start.2
  813.0 9.6 copy-start.57
  829.0 8.7 copy-start.17
  829.0 170.9 %all-reduce.14.cloned.1.call-start = ((), (), s32[]{:S(2)}) async-start(), calls=%async_computation.6 | async-start | bytes 12582912 | tf_op jit(solution)/shard_map/psum | solution.py:227
  879.9 363.2 %all-reduce.12.cloned.1.call-start = ((), (), s32[]{:S(2)}) async-start(), calls=%async_computation.5 | async-start | bytes 14155776 | tf_op jit(solution)/shard_map/psum | solution.py:275
  880.2 15.8 %slice-start = ((s8[6291456]{0:T(1024)(128)(4,1)}), s8[4194304]{0:T(1024)(128)(4,1)S(1)}, s32[]{:S(2)}) async-start(s8[6291456]{0:T(1024)(128)(4,1)} %bitcast.206), calls=%async_computation.7 | async-start | bytes 8388608
  887.3 7.9 copy-start.10
  887.3 8.7 slice-start.1
  887.3 8.7 copy-start.23
  899.3 100.6 %copy-start.32 = (f32[2048]{0:T(1024)S(1)}, f32[2048]{0:T(1024)}, u32[]{:S(2)}) copy-start(f32[2048]{0:T(1024)} %copy-done.31) | copy-start | bytes 24580
  899.3 100.6 %copy-start.35 = (f32[768]{0:T(1024)S(1)}, f32[768]{0:T(1024)}, u32[]{:S(2)}) copy-start(f32[768]{0:T(1024)} %param.22) | copy-start | bytes 9220
  899.3 100.6 %copy-start.41 = (f32[768]{0:T(1024)S(1)}, f32[768]{0:T(1024)}, u32[]{:S(2)}) copy-start(f32[768]{0:T(1024)} %param.23) | copy-start | bytes 9220
  901.4 103.8 %copy-start.37 = (f32[2048]{0:T(1024)S(1)}, f32[2048]{0:T(1024)}, u32[]{:S(2)}) copy-start(f32[2048]{0:T(1024)} %copy-done.36) | copy-start | bytes 24580
  1005.4 49.8 %copy-start.48 = (f32[768]{0:T(1024)S(1)}, f32[768]{0:T(1024)}, u32[]{:S(2)}) copy-start(f32[768]{0:T(1024)} %param.34) | copy-start | bytes 9220
  (48 other events, 198.7 us)
Sparse Core Ops, SparseCore 0:
  19.9 47.6 all-gather.1
  262.7 68.4 all-reduce.7
  353.9 68.5 all-reduce.9
  829.1 43.4 reduce-scatter.1
  880.1 119.7 all-reduce.13
  1005.9 237.1 all-reduce.11
where the time goes:
time: 1270 us; the launch traced here: 1260 us
  waiting for transfers between devices  493 us (39%)
  matrix products  449 us (35%)
  other arithmetic  193 us (15%)
  local copies, waits for them, and re-layouts  48.5 us (4%)
  blocking collectives  41.2 us (3%)
  loops' own time  17.1 us (1%)
  between operations  15 us (1%)
    psum x1, waiting for transfers between devices, local(): lax.psum((grad_w_qkv, grad_b_qv, grad_w_out, grad_w_up, grad_b_up, grad_w...  185 us
    dot_general x8, matrix products, one_block(): jnp.einsum('qhd,khd->hqk', q_block, key_heads, preferred_element_type=jnp...  101 us
    psum x1, waiting for transfers between devices, local(): lax.psum(partial_mlp.astype(jnp.bfloat16), 'tensor').astype(jnp.float32)  97.5 us
    convert_element_type x4, other arithmetic, one_block(): grad_score = (probs_full * (grad_prob - inner)).astype(jnp.bfloat16)  87.6 us
    dot_general x4, matrix products, one_block(): jnp.einsum('qhd,khd->hqk', g_block, value_heads, preferred_element_type=j...  73.2 us
    psum x1, waiting for transfers between devices, local(): lax.psum(partial_lift.astype(jnp.bfloat16), 'tensor').astype(jnp.float32)  68.6 us
    psum x1, waiting for transfers between devices, local(): lax.psum(partial_attn.astype(jnp.bfloat16), 'tensor').astype(jnp.float32)  68.4 us
    dot_general x4, matrix products, one_block(): jnp.einsum('hqk,qhd->khd', probs_full.astype(jnp.bfloat16), g_block, pref...  53.5 us
  transfers between devices with their start and end apart: 6, of which 6 were waited for; matrix products, arithmetic and copies ran while one was open for 5% of the time, Pallas kernels for 0%

commit v1 on v0

--- a/solution.py
+++ b/solution.py
@@ -273,22 +273,25 @@
     grad_g1 = row_total(grad_norm * norm_one)
     grad_b1 = row_total(grad_norm)
     summed = lax.psum(
-        (
-            grad_w_qkv,
-            grad_b_qv,
-            grad_w_out,
-            grad_w_up,
-            grad_b_up,
-            grad_w_down,
-            grad_b_down,
-            grad_pass,
-            grad_g1,
-            grad_b1,
-            grad_g2,
-            grad_b2,
-            grad_b_out,
+        lax.psum(
+            (
+                grad_w_qkv,
+                grad_b_qv,
+                grad_w_out,
+                grad_w_up,
+                grad_b_up,
+                grad_w_down,
+                grad_b_down,
+                grad_pass,
+                grad_g1,
+                grad_b1,
+                grad_g2,
+                grad_b2,
+                grad_b_out,
+            ),
+            "seq",
         ),
-        ("dp", "seq"),
+        "dp",
     )
     return (
         output,

time: 1270 us -> 1450 us (1.14)
  waiting for transfers between devices: 493 us -> 687 us
    psum x0 -> x1, waiting for transfers between devices: none -> 204 us  [local(): lax.psum(lax.psum((grad_w_qkv, grad_b_qv, grad_w_out, grad_w_up, grad_b_u...]
    psum x1, blocking collectives: 41.2 us -> 8.51 us  [local(): lax.psum((grad_w_qkv, grad_b_qv, grad_w_out, grad_w_up, grad_b_up, grad_w...]
    psum x1, waiting for transfers between devices: 185 us -> 157 us  [local(): lax.psum((grad_w_qkv, grad_b_qv, grad_w_out, grad_w_up, grad_b_up, grad_w...]
    psum x0 -> x1, blocking collectives: none -> 24.2 us  [local(): lax.psum(lax.psum((grad_w_qkv, grad_b_qv, grad_w_out, grad_w_up, grad_b_u...]
    psum x1, waiting for transfers between devices: 97.5 us -> 120 us  [local(): lax.psum(partial_mlp.astype(jnp.bfloat16), 'tensor').astype(jnp.float32)]
  transfers between devices with their start and end apart: 6 -> 7, of which waited for: 6 -> 7; matrix products, arithmetic and copies ran while one was open for 5% -> 4% of each run, Pallas kernels for 0% -> 0%
where the time goes in v1:
time: 1450 us; the launch traced here: 1440 us
  waiting for transfers between devices  687 us (47%)
  matrix products  448 us (31%)
  other arithmetic  194 us (13%)
  local copies, waits for them, and re-layouts  47.7 us (3%)
  blocking collectives  32.7 us (2%)
  loops' own time  17.1 us (1%)
  between operations  15.1 us (1%)
    psum x1, waiting for transfers between devices, local(): lax.psum(lax.psum((grad_w_qkv, grad_b_qv, grad_w_out, grad_w_up, grad_b_u...  204 us
    psum x1, waiting for transfers between devices, local(): lax.psum((grad_w_qkv, grad_b_qv, grad_w_out, grad_w_up, grad_b_up, grad_w...  157 us
    psum x1, waiting for transfers between devices, local(): lax.psum(partial_mlp.astype(jnp.bfloat16), 'tensor').astype(jnp.float32)  120 us
    dot_general x8, matrix products, one_block(): jnp.einsum('qhd,khd->hqk', q_block, key_heads, preferred_element_type=jnp...  101 us
    convert_element_type x4, other arithmetic, one_block(): grad_score = (probs_full * (grad_prob - inner)).astype(jnp.bfloat16)  87.6 us
    dot_general x4, matrix products, one_block(): jnp.einsum('qhd,khd->hqk', g_block, value_heads, preferred_element_type=j...  73.2 us
    psum x1, waiting for transfers between devices, local(): lax.psum(partial_lift.astype(jnp.bfloat16), 'tensor').astype(jnp.float32)  68.6 us
    psum x1, waiting for transfers between devices, local(): lax.psum(partial_attn.astype(jnp.bfloat16), 'tensor').astype(jnp.float32)  68.4 us
  transfers between devices with their start and end apart: 7, of which 7 were waited for; matrix products, arithmetic and copies ran while one was open for 4% of the time, Pallas kernels for 0%

profile of v1, /device:TPU:0, one launch (start us, length us, event | category | flops | bytes accessed | tf_op | source)
XLA Modules:
  0.0 1441.7 jit_solution(8261019158202671147)
XLA Ops:
  23.9 43.7 %all-gather.2.cloned.1.call-done = bf16[1,4096,384]{1,2,0:T(8,128)(2,1)} async-done(((bf16[1,2048,384]{1,2,0:T(8,128)(2,1)}), bf16[1,4096,384]{1,2,0:T(8,128)(2,1)}) %all-gather.2.cloned.1.call-update) | async-done | bytes 3145744 | tf_op jit(solution)/shard_map/all_gather | solution.py:199
  71.8 184.3 %while.27 = (s32[]{:T(128)}, bf16[4,512,3,64]{1,3,2,0:T(8,128)(2,1)}, f32[4,3,512]{2,1,0:T(4,128)}, s32[4]{0:T(128)S(1)}, s32[4096]{0:T(1024)}, /*index=5*/s32[1...) while((s32[]{:T(128)}, ...), condition=%wide.region_5.6_spmd, body=%wide.region_2.5_spmd.sunk | while | flops 1751353856 | bytes 108675712 | solution.py:101
  81.2 12.1 fusion.191
  93.2 12.0 fusion.192
  105.2 12.1 fusion.193
  127.1 12.1 fusion.191
  139.2 12.0 fusion.192
  151.2 12.1 fusion.193
  173.1 12.1 fusion.191
  185.1 12.0 fusion.192
  197.1 12.1 fusion.193
  219.0 12.1 fusion.191
  231.1 12.0 fusion.192
  243.1 12.1 fusion.193
  262.8 68.4 %all-reduce.11.cloned.1.call-done = bf16[1,2048,768]{2,1,0:T(8,128)(2,1)} async-done(((bf16[1,2048,768]{2,1,0:T(8,128)(2,1)}), bf16[1,2048,768]{2,1,0:T(8,128)(2,1)}) %all-reduce.11.cloned.1.call-update) | async-done | bytes 3145744 | tf_op jit(solution)/shard_map/psum | solution.py:218
  353.9 68.6 %all-reduce.13.cloned.1.call-done = bf16[1,2048,768]{2,1,0:T(8,128)(2,1)} async-done(((bf16[1,2048,768]{2,1,0:T(8,128)(2,1)}), bf16[1,2048,768]{2,1,0:T(8,128)(2,1)}) %all-reduce.13.cloned.1.call-update) | async-done | bytes 3145744 | tf_op jit(solution)/shard_map/psum | solution.py:235
  445.2 377.5 %while.28 = (s32[]{:T(128)}, f32[4096,3,64]{0,2,1:T(8,128)}, f32[4096,3,64]{0,2,1:T(8,128)}, bf16[4,512,3,64]{1,3,2,0:T(8,128)(2,1)}, bf16[4,512,3,64]{1,3,2,0:T...) while((s32[]{:T(128)}, f32[4096,3,64]{0,2,1:T(8,128)}, ...), condition=%wide.region_15.16_spmd.clone, body=%wide.region_13.15_spmd.clone.sunk | while | flops 4190177792 | bytes 234558224 | solution.py:152
  453.9 13.3 fusion.205
  467.2 12.5 fusion.208
  479.8 18.3 %multiply_reduce_fusion.4 = (f32[3,512]{1,0:T(4,128)S(1)}, f32[3,512,4096]{2,1,0:T(8,128)}) fusion(f32[3,512,4096]{2,1,0:T(8,128)} %fusion.205, f32[3,512]{1,0:T(4,128)S(1)} %dynamic-slice_bitcast_fusion.2, pred[512,4096]{1,0:T(8,128)(4,1)S(1)} %fusion.206, bf16[4096,3,64]{0,2,1:T(8,128)(2,1)} %get-tuple-element.564, ...), kind=kOutput, calls=%fused_computation.25.clone.1 | convolution fusion | flops 836762112 | bytes 54210564 | tf_op jit(solution)/shard_map/while/body/eval_jaxpr/qhd,khd->hqk/dot_general | solution.py:127
  498.1 21.9 %multiply_convert_fusion.5 = bf16[3,512,4096]{2,1,0:T(8,128)(2,1)} fusion(f32[3,512,4096]{2,1,0:T(8,128)} %get-tuple-element.479, f32[3,512,4096]{2,1,0:T(8,128)} %fusion.205, f32[3,512]{1,0:T(4,128)S(1)} %get-tuple-element.480, f32[3,512]{1,0:T(4,128)S(1)} %dynamic-slice_bitcast_fusion.2, pred[512,4096]{1,0:T(8,128)(4,1)S(1)} %fusion.206), kind=kLoop, calls=%fused_computation.24.clone.1 | loop fusion | flops 37748736 | bytes 65024000 | tf_op jit(solution)/shard_map/while/body/eval_jaxpr/convert_element_type | solution.py:131
  520.0 9.7 fusion.209
  529.7 8.7 fusion.207
  546.7 13.3 fusion.205
  560.0 13.6 fusion.208
  573.6 18.3 %multiply_reduce_fusion.4 = (f32[3,512]{1,0:T(4,128)S(1)}, f32[3,512,4096]{2,1,0:T(8,128)}) fusion(f32[3,512,4096]{2,1,0:T(8,128)} %fusion.205, f32[3,512]{1,0:T(4,128)S(1)} %dynamic-slice_bitcast_fusion.2, pred[512,4096]{1,0:T(8,128)(4,1)S(1)} %fusion.206, bf16[4096,3,64]{0,2,1:T(8,128)(2,1)} %get-tuple-element.564, ...), kind=kOutput, calls=%fused_computation.25.clone.1 | convolution fusion | flops 836762112 | bytes 54210564 | tf_op jit(solution)/shard_map/while/body/eval_jaxpr/qhd,khd->hqk/dot_general | solution.py:127
  591.9 21.9 %multiply_convert_fusion.5 = bf16[3,512,4096]{2,1,0:T(8,128)(2,1)} fusion(f32[3,512,4096]{2,1,0:T(8,128)} %get-tuple-element.479, f32[3,512,4096]{2,1,0:T(8,128)} %fusion.205, f32[3,512]{1,0:T(4,128)S(1)} %get-tuple-element.480, f32[3,512]{1,0:T(4,128)S(1)} %dynamic-slice_bitcast_fusion.2, pred[512,4096]{1,0:T(8,128)(4,1)S(1)} %fusion.206), kind=kLoop, calls=%fused_computation.24.clone.1 | loop fusion | flops 37748736 | bytes 65024000 | tf_op jit(solution)/shard_map/while/body/eval_jaxpr/convert_element_type | solution.py:131
  613.8 9.7 fusion.209
  623.5 9.6 fusion.207
  641.5 13.3 fusion.205
  654.7 13.6 fusion.208
  668.4 18.3 %multiply_reduce_fusion.4 = (f32[3,512]{1,0:T(4,128)S(1)}, f32[3,512,4096]{2,1,0:T(8,128)}) fusion(f32[3,512,4096]{2,1,0:T(8,128)} %fusion.205, f32[3,512]{1,0:T(4,128)S(1)} %dynamic-slice_bitcast_fusion.2, pred[512,4096]{1,0:T(8,128)(4,1)S(1)} %fusion.206, bf16[4096,3,64]{0,2,1:T(8,128)(2,1)} %get-tuple-element.564, ...), kind=kOutput, calls=%fused_computation.25.clone.1 | convolution fusion | flops 836762112 | bytes 54210564 | tf_op jit(solution)/shard_map/while/body/eval_jaxpr/qhd,khd->hqk/dot_general | solution.py:127
  686.7 21.9 %multiply_convert_fusion.5 = bf16[3,512,4096]{2,1,0:T(8,128)(2,1)} fusion(f32[3,512,4096]{2,1,0:T(8,128)} %get-tuple-element.479, f32[3,512,4096]{2,1,0:T(8,128)} %fusion.205, f32[3,512]{1,0:T(4,128)S(1)} %get-tuple-element.480, f32[3,512]{1,0:T(4,128)S(1)} %dynamic-slice_bitcast_fusion.2, pred[512,4096]{1,0:T(8,128)(4,1)S(1)} %fusion.206), kind=kLoop, calls=%fused_computation.24.clone.1 | loop fusion | flops 37748736 | bytes 65024000 | tf_op jit(solution)/shard_map/while/body/eval_jaxpr/convert_element_type | solution.py:131
  708.6 9.7 fusion.209
  718.3 9.6 fusion.207
  736.2 13.3 fusion.205
  749.5 13.6 fusion.208
  763.1 18.3 %multiply_reduce_fusion.4 = (f32[3,512]{1,0:T(4,128)S(1)}, f32[3,512,4096]{2,1,0:T(8,128)}) fusion(f32[3,512,4096]{2,1,0:T(8,128)} %fusion.205, f32[3,512]{1,0:T(4,128)S(1)} %dynamic-slice_bitcast_fusion.2, pred[512,4096]{1,0:T(8,128)(4,1)S(1)} %fusion.206, bf16[4096,3,64]{0,2,1:T(8,128)(2,1)} %get-tuple-element.564, ...), kind=kOutput, calls=%fused_computation.25.clone.1 | convolution fusion | flops 836762112 | bytes 54210564 | tf_op jit(solution)/shard_map/while/body/eval_jaxpr/qhd,khd->hqk/dot_general | solution.py:127
  781.4 21.9 %multiply_convert_fusion.5 = bf16[3,512,4096]{2,1,0:T(8,128)(2,1)} fusion(f32[3,512,4096]{2,1,0:T(8,128)} %get-tuple-element.479, f32[3,512,4096]{2,1,0:T(8,128)} %fusion.205, f32[3,512]{1,0:T(4,128)S(1)} %get-tuple-element.480, f32[3,512]{1,0:T(4,128)S(1)} %dynamic-slice_bitcast_fusion.2, pred[512,4096]{1,0:T(8,128)(4,1)S(1)} %fusion.206), kind=kLoop, calls=%fused_computation.24.clone.1 | loop fusion | flops 37748736 | bytes 65024000 | tf_op jit(solution)/shard_map/while/body/eval_jaxpr/convert_element_type | solution.py:131
  803.3 9.7 fusion.209
  813.0 9.6 fusion.207
  847.4 25.2 %reduce-scatter.2.cloned.1.call-done = bf16[1,2048,384]{1,2,0:T(8,128)(2,1)} async-done(((bf16[1,4096,384]{1,2,0:T(8,128)(2,1)}), bf16[1,2048,384]{1,2,0:T(8,128)(2,1)}) %reduce-scatter.2.cloned.1.call-update) | async-done | bytes 1572880 | tf_op jit(solution)/shard_map/reduce_scatter | solution.py:256
  880.0 8.6 fusion.90
  894.0 157.1 %all-reduce.17.cloned.1.call-done = (f32[3,768,192]{1,2,0:T(8,128)}, f32[192,768]{1,0:T(8,128)}, f32[768,768]{1,0:T(8,128)}, f32[768,768]{1,0:T(8,128)}) async-done(((f32[3,768,192]{1,2,0:T(8,128)}, f32[192,768]{1,0:T(8,128)}, f32[768,768]{1,0:T(8,128)}, f32[768,768]{1,0:T(8,128)}), (f32[3,768,192]{1,2,0:T(8,128)}, f32[192,768]{1,0:T(8,128)}, f32[768,768]{1,0:T(8,128)}, ...) | async-done | bytes 7077904 | tf_op jit(solution)/shard_map/psum | solution.py:276
  1053.0 120.3 %all-reduce.19.cloned.1.call-done = (bf16[1,2048,768]{2,1,0:T(8,128)(2,1)}, bf16[1,2048,768]{2,1,0:T(8,128)(2,1)}) async-done(((bf16[1,2048,768]{2,1,0:T(8,128)(2,1)}, bf16[1,2048,768]{2,1,0:T(8,128)(2,1)}), (bf16[1,2048,768]{2,1,0:T(8,128)(2,1)}, bf16[1,2048,768]{2,1,0:T(8,128)(2,1)})) %all-reduce.19.cloned.1.call-update) | async-done | bytes 6291472 | tf_op jit(solution)/shard_map/psum | solution.py:227
  1186.0 8.5 all-reduce.2
  1194.5 24.2 %all-reduce = (f32[768]{0:T(1024)}, f32[768]{0:T(1024)}, f32[768]{0:T(1024)}, f32[2,192]{1,0:T(2,128)}, f32[768]{0:T(1024)}, /*index=5*/f32[768]{0:T(1024)}, f32[768]{0:T(1024)}, f32[768]{0:T(1024)}, f32[768]{0:T(1024)}) all-reduce(f32[768]{0:T(1024)S(1)} %get-tuple-element.297, ...), channel_id=1, replica_groups=mesh['dp'=4,'seq'=2,'tensor'=4] {'dp'}, use_global_device_ids=true, to_apply=%region_22.23 | all-reduce | flops 6528 | bytes 52224 | tf_op jit(solution)/shard_map/psum | solution.py:275
  1223.4 203.5 %all-reduce.15.cloned.1.call-done = (f32[3,768,192]{1,2,0:T(8,128)}, f32[192,768]{1,0:T(8,128)}, f32[768,768]{1,0:T(8,128)}, f32[768,768]{1,0:T(8,128)}) async-done(((f32[3,768,192]{1,2,0:T(8,128)}, f32[192,768]{1,0:T(8,128)}, f32[768,768]{1,0:T(8,128)}, f32[768,768]{1,0:T(8,128)}), (f32[3,768,192]{1,2,0:T(8,128)}, f32[192,768]{1,0:T(8,128)}, f32[768,768]{1,0:T(8,128)}, ...) | async-done | bytes 7077904 | tf_op jit(solution)/shard_map/psum | solution.py:275
  (301 shorter events, 193.3 us)
Async XLA Ops:
  7.2 334.1 %copy-start = (bf16[768,768]{1,0:T(8,128)(2,1)S(1)}, bf16[768,768]{1,0:T(8,128)(2,1)}, u32[]{:S(2)}) copy-start(bf16[768,768]{1,0:T(8,128)(2,1)} %param.33) | copy-start | bytes 3538948
  7.2 60.3 %all-gather.2.cloned.1.call-start = ((), (), s32[]{:S(2)}) async-start(), calls=%async_computation.1 | async-start | bytes 4718592 | tf_op jit(solution)/shard_map/all_gather | solution.py:199
  19.8 311.5 %all-reduce.11.cloned.1.call-start = ((), (), s32[]{:S(2)}) async-start(), calls=%async_computation.2 | async-start | bytes 6291456 | tf_op jit(solution)/shard_map/psum | solution.py:218
  81.1 12.1 copy-start.8
  93.2 12.0 copy-start.7
  93.2 12.0 copy-start.23
  127.1 12.1 copy-start.8
  139.2 12.0 copy-start.7
  139.2 12.0 copy-start.23
  173.1 12.1 copy-start.8
  185.1 12.0 copy-start.7
  185.1 12.0 copy-start.23
  219.0 12.1 copy-start.8
  231.1 12.0 copy-start.7
  231.1 12.0 copy-start.23
  256.1 79.3 %copy-start.55 = (s32[4]{0:T(128)}, s32[4]{0:T(128)S(1)}, u32[]{:S(2)}) copy-start(s32[4]{0:T(128)S(1)} %get-tuple-element.649) | copy-start | bytes 52
  256.1 79.3 %copy-start.58 = (bf16[13,13]{1,0:T(8,128)(2,1)}, bf16[13,13]{1,0:T(8,128)(2,1)S(1)}, u32[]{:S(2)}) copy-start(bf16[13,13]{1,0:T(8,128)(2,1)S(1)} %get-tuple-element.667) | copy-start | bytes 1018
  256.1 75.2 %copy-start.34 = (f32[768]{0:T(1024)S(1)}, f32[768]{0:T(1024)}, u32[]{:S(2)}) copy-start(f32[768]{0:T(1024)} %param.22) | copy-start | bytes 9220
  256.1 75.2 %copy-start.46 = (f32[768]{0:T(1024)S(1)}, f32[768]{0:T(1024)}, u32[]{:S(2)}) copy-start(f32[768]{0:T(1024)} %param.28) | copy-start | bytes 9220
  262.6 159.9 %all-reduce.13.cloned.1.call-start = ((), (), s32[]{:S(2)}) async-start(), calls=%async_computation.3 | async-start | bytes 6291456 | tf_op jit(solution)/shard_map/psum | solution.py:235
  353.8 518.8 %reduce-scatter.2.cloned.1.call-start = ((), (), s32[]{:S(2)}) async-start(), calls=%async_computation.4 | async-start | bytes 4718592 | tf_op jit(solution)/shard_map/reduce_scatter | solution.py:256
  428.5 8.6 copy-start.30
  434.5 10.8 copy-start.56
  520.0 9.7 copy-start.15
  529.6 8.7 copy-start.2
  529.6 8.7 copy-start.57
  613.8 9.7 copy-start.15
  623.5 9.6 copy-start.2
  623.5 9.6 copy-start.57
  708.6 9.7 copy-start.15
  718.3 9.6 copy-start.2
  718.3 9.6 copy-start.57
  803.3 9.7 copy-start.15
  813.0 9.6 copy-start.2
  813.0 9.6 copy-start.57
  829.0 222.2 %all-reduce.17.cloned.1.call-start = ((), (), s32[]{:S(2)}) async-start(), calls=%async_computation.6 | async-start | bytes 14155776 | tf_op jit(solution)/shard_map/psum | solution.py:276
  829.0 16.7 %slice-start = ((s8[6291456]{0:T(1024)(128)(4,1)}), s8[4194304]{0:T(1024)(128)(4,1)S(1)}, s32[]{:S(2)}) async-start(s8[6291456]{0:T(1024)(128)(4,1)} %bitcast.206), calls=%async_computation.8 | async-start | bytes 8388608
  836.1 8.7 copy-start.10
  836.2 9.6 slice-start.1
  879.8 293.5 %all-reduce.19.cloned.1.call-start = ((), (), s32[]{:S(2)}) async-start(), calls=%async_computation.7 | async-start | bytes 12582912 | tf_op jit(solution)/shard_map/psum | solution.py:227
  880.0 8.7 copy-start.29
  893.9 157.3 %copy-start.17 = (bf16[4,512,3,64]{1,3,2,0:T(8,128)(2,1)S(1)}, bf16[4,512,3,64]{1,3,2,0:T(8,128)(2,1)}, u32[]{:S(2)}) copy-start(bf16[4,512,3,64]{1,3,2,0:T(8,128)(2,1)} %get-tuple-element.653) | copy-start | bytes 2359300
  893.9 279.3 %copy-start.32 = (f32[2048]{0:T(1024)S(1)}, f32[2048]{0:T(1024)}, u32[]{:S(2)}) copy-start(f32[2048]{0:T(1024)} %copy-done.31) | copy-start | bytes 24580
  893.9 279.3 %copy-start.35 = (f32[768]{0:T(1024)S(1)}, f32[768]{0:T(1024)}, u32[]{:S(2)}) copy-start(f32[768]{0:T(1024)} %param.22) | copy-start | bytes 9220
  893.9 279.3 %copy-start.41 = (f32[768]{0:T(1024)S(1)}, f32[768]{0:T(1024)}, u32[]{:S(2)}) copy-start(f32[768]{0:T(1024)} %param.23) | copy-start | bytes 9220
  894.0 533.0 %all-reduce.15.cloned.1.call-start = ((), (), s32[]{:S(2)}) async-start(), calls=%async_computation.5 | async-start | bytes 14155776 | tf_op jit(solution)/shard_map/psum | solution.py:275
  1052.0 126.7 %copy-start.37 = (f32[2048]{0:T(1024)S(1)}, f32[2048]{0:T(1024)}, u32[]{:S(2)}) copy-start(f32[2048]{0:T(1024)} %copy-done.36) | copy-start | bytes 24580
  1178.7 42.0 %copy-start.48 = (f32[768]{0:T(1024)S(1)}, f32[768]{0:T(1024)}, u32[]{:S(2)}) copy-start(f32[768]{0:T(1024)} %param.34) | copy-start | bytes 9220
  (49 other events, 216.0 us)
Sparse Core Ops, SparseCore 0:
  19.9 47.6 all-gather.1
  262.7 68.4 all-reduce.10
  353.9 68.5 all-reduce.12
  829.1 43.4 reduce-scatter.1
  879.9 171.2 all-reduce.16
  1053.4 119.7 all-reduce.18
  1175.9 251.0 all-reduce.14
